TPU v7x, 32 devices: a whole 2x2x4 slice. The times are simulated.
32 devices in a mesh: pix: 16 (over z, y, core), chan: 2 (over x).
Axes of the slice: x: 2, y: 2, z: 4, core: 2. Of those that a mesh axis runs over, the one named last changes fastest.
Arguments:
- spectra: float32 [32768, 4096], P('pix', 'chan'), may hold values from 0.1 to 3
- coeffs: float32 [32, 32768], P(None, 'pix'), may hold values from 0.05 to 0.5
- endmembers: float32 [32, 4096], P(None, 'chan'), may hold values from 0.05 to 0.5
- pixel_mask: int32 [32768], P('pix'), may hold values from 0 to 1
- labels: int32 [32768], P('pix'), may hold values from 0 to 23
Outputs:
- new_coeffs: float32 [32, 32768], P(None, 'pix')
- new_endmembers: float32 [32, 4096], P(None, 'chan')
- centroids: float32 [24, 4096], P(None, 'chan')
- distances: float32 [32768], P('pix')
All inputs are finite; a program needn't handle non-finite values.
Results may differ from a plain program's by a relative error of at most 0.0003.
Values sent between devices are 32-bit elements; how exact they have to be, the bound alone decides.
No kernel may reach another device: no remote copies, remote signals or barrier semaphores. Data moves between devices by JAX's collectives and lax.ppermute only.
A program may use at most 64 MiB of HBM per device.

v0:
```python
import jax
import jax.numpy as jnp
from jax import lax
from jax.sharding import PartitionSpec as P

PHASES = 24
EPSILON = 1e-06


def product(left, right):
    return jnp.dot(left, right, precision=lax.Precision.HIGHEST, preferred_element_type=jnp.float32)


def contract(left, right, left_dim, right_dim):
    return lax.dot_general(
        left,
        right,
        (((left_dim,), (right_dim,)), ((), ())),
        precision=lax.Precision.HIGHEST,
        preferred_element_type=jnp.float32,
    )


def local(spectra, coeffs, endmembers, pixel_mask, labels):
    channels_total = endmembers.shape[1] * lax.axis_size("chan")
    local_numer = contract(endmembers, spectra, 1, 1)
    local_gram = contract(endmembers, endmembers, 1, 1)
    numer_coeff, gram_all = lax.psum((local_numer, local_gram), "chan")
    new_coeffs = coeffs * numer_coeff / (product(gram_all, coeffs) + EPSILON)
    weights = pixel_mask.astype(jnp.float32)
    weighted = new_coeffs * weights[None, :]
    onehot = (labels[None, :] == jnp.arange(PHASES, dtype=jnp.int32)[:, None]).astype(jnp.float32)
    picked = onehot * weights[None, :]
    numer_end, outer_gram, phase_sums, phase_counts = lax.psum(
        (
            product(weighted, spectra),
            contract(weighted, new_coeffs, 1, 1),
            contract(picked, new_coeffs, 1, 1),
            jnp.sum(picked, axis=1),
        ),
        "pix",
    )
    new_endmembers = endmembers * numer_end / (product(outer_gram, endmembers) + EPSILON)
    phase_means = phase_sums / (phase_counts + 1.0)[:, None]
    centroids = product(phase_means, new_endmembers)
    gram_updated = lax.psum(contract(new_endmembers, new_endmembers, 1, 1), "chan")
    offset = new_coeffs - contract(phase_means, onehot, 0, 0)
    distance = jnp.sum(offset * product(gram_updated, offset), axis=0) / channels_total
    return (new_coeffs, new_endmembers, centroids, distance)


def solution(mesh):
    placed = (P("pix", "chan"), P(None, "pix"), P(None, "chan"), P("pix"), P("pix"))
    return jax.shard_map(
        local,
        mesh=mesh,
        in_specs=placed,
        out_specs=(P(None, "pix"), P(None, "chan"), P(None, "chan"), P("pix")),
        check_vma=False,
    )
```

profile of v0, /device:TPU:0, one launch (start us, length us, event | category | flops | bytes accessed | tf_op | source)
XLA Modules:
  0.0 179.4 jit_solution(9026116440240854238)
XLA Ops:
  7.2 0.0 all-reduce.4.cloned.1.call-start
  7.3 21.4 %fusion.17 = f32[32,2048]{1,0:T(8,128)} fusion(f32[32,2048]{1,0:T(8,128)} %param.7, f32[2048,2048]{1,0:T(8,128)} %param.5), kind=kOutput, calls=%fused_computation.26 | convolution fusion | flops 1610612736 | bytes 17301504 | tf_op jit(solution)/shard_map/dot_general | solution.py:15
  28.6 0.0 all-reduce.4.cloned.1.call-update
  28.7 0.0 all-reduce.6.cloned.1.call-start
  28.7 0.4 fusion.18
  29.1 9.7 %psum.50 = f32[32,32]{1,0:T(8,128)S(1)} all-reduce(f32[32,32]{1,0:T(8,128)S(1)} %fusion.18), channel_id=1, replica_groups=mesh['pix'=16,'chan'=2] {'chan'}, use_global_device_ids=true, to_apply=%region_1.0 | all-reduce | flops 1024 | bytes 8192 | tf_op jit(solution)/shard_map/psum | solution.py:28
  38.8 0.1 select_reduce_fusion
  38.9 16.0 %all-reduce.4.cloned.1.call-done = f32[32,2048]{1,0:T(8,128)} async-done(((f32[32,2048]{1,0:T(8,128)}), f32[32,2048]{1,0:T(8,128)}) %all-reduce.4.cloned.1.call-update) | async-done | bytes 262160 | tf_op jit(solution)/shard_map/psum | solution.py:28
  54.9 1.3 fusion.1
  56.3 0.0 copy-start
  56.3 0.3 fusion.3
  56.6 0.3 fusion.7
  56.9 13.9 %fusion.5 = f32[32,2048]{1,0:T(8,128)} fusion(f32[2048,2048]{1,0:T(8,128)} %param.5, f32[32,2048]{1,0:T(8,128)S(1)} %fusion.1, f32[2048]{0:T(1024)S(1)} %convert_element_type.4), kind=kOutput, calls=%fused_computation.9 | convolution fusion | flops 1610678272 | bytes 17309696 | tf_op jit(solution)/shard_map/dot_general | solution.py:11
  70.8 0.0 all-reduce.6.cloned.1.call-update
  70.8 60.7 %all-reduce = (f32[32,32]{1,0:T(8,128)S(1)}, f32[24,32]{1,0:T(8,128)S(1)}, f32[24]{0:T(128)S(1)}) all-reduce(f32[32,32]{1,0:T(8,128)S(1)} %fusion.3, f32[24,32]{1,0:T(8,128)S(1)} %fusion.7, f32[24]{0:T(128)S(1)} %select_reduce_fusion), channel_id=1, replica_groups=mesh['pix'=16,'chan'=2] {'pix'}, use_global_device_ids=true, to_apply=%region_3.0 | all-reduce | flops 1816 | bytes 14528 | tf_op jit(solution)/shard_map/psum | solution.py:34
  131.5 0.4 convolution_subtract_fusion
  131.9 28.7 %all-reduce.6.cloned.1.call-done = f32[32,2048]{1,0:T(8,128)} async-done(((f32[32,2048]{1,0:T(8,128)}), f32[32,2048]{1,0:T(8,128)}) %all-reduce.6.cloned.1.call-update) | async-done | bytes 262160 | tf_op jit(solution)/shard_map/psum | solution.py:34
  160.7 1.3 fusion
  162.0 0.0 copy-start.2
  162.0 1.1 fusion.15
  163.1 0.4 fusion.19
  163.4 8.1 %psum.55 = f32[32,32]{1,0:T(8,128)S(1)} all-reduce(f32[32,32]{1,0:T(8,128)S(1)} %fusion.19), channel_id=1, replica_groups=mesh['pix'=16,'chan'=2] {'chan'}, use_global_device_ids=true, to_apply=%region_7.0 | all-reduce | flops 1024 | bytes 8192 | tf_op jit(solution)/shard_map/psum | solution.py:46
  171.5 0.4 fusion.2
  171.9 0.6 broadcast_multiply_fusion
  (12 shorter events, 0.0 us)
Async XLA Ops:
  7.2 21.6 %copy-start.1 = (f32[32,2048]{1,0:T(8,128)S(1)}, f32[32,2048]{1,0:T(8,128)}, u32[]{:S(2)}) copy-start(f32[32,2048]{1,0:T(8,128)} %param.7) | copy-start | bytes 786436
  7.2 21.5 %copy-start.4 = (s32[2048]{0:T(1024)S(1)}, s32[2048]{0:T(1024)}, u32[]{:S(2)}) copy-start(s32[2048]{0:T(1024)} %param.8) | copy-start | bytes 24580
  7.2 31.6 %copy-start.3 = (s32[2048]{0:T(1024)S(1)}, s32[2048]{0:T(1024)}, u32[]{:S(2)}) copy-start(s32[2048]{0:T(1024)} %param.9) | copy-start | bytes 24580
  7.2 47.7 %copy-start.5 = (f32[32,2048]{1,0:T(8,128)S(1)}, f32[32,2048]{1,0:T(8,128)}, u32[]{:S(2)}) copy-start(f32[32,2048]{1,0:T(8,128)} %param.6) | copy-start | bytes 786436
  7.2 47.7 %all-reduce.4.cloned.1.call-start = ((), (), s32[]{:S(2)}) async-start(), calls=%async_computation | async-start | bytes 524288 | tf_op jit(solution)/shard_map/psum | solution.py:28
  28.7 132.0 %all-reduce.6.cloned.1.call-start = ((), (), s32[]{:S(2)}) async-start(), calls=%async_computation.1 | async-start | bytes 524288 | tf_op jit(solution)/shard_map/psum | solution.py:34
  56.3 116.3 %copy-start = (f32[32,2048]{1,0:T(8,128)}, f32[32,2048]{1,0:T(8,128)S(1)}, u32[]{:S(2)}) copy-start(f32[32,2048]{1,0:T(8,128)S(1)} %fusion.1) | copy-start | bytes 786436
  162.0 10.5 %copy-start.2 = (f32[32,2048]{1,0:T(8,128)}, f32[32,2048]{1,0:T(8,128)S(1)}, u32[]{:S(2)}) copy-start(f32[32,2048]{1,0:T(8,128)S(1)} %fusion) | copy-start | bytes 786436
Sparse Core Ops, SparseCore 0:
  28.8 26.0 all-reduce.3
  70.9 89.7 all-reduce.5
where the time goes:
time: 180 us; the launch traced here: 179 us
  blocking collectives  78.5 us (44%)
  waiting for transfers between devices  44.8 us (25%)
  matrix products  41 us (23%)
  between operations  14.2 us (8%)
    psum x1, blocking collectives, local(): lax.psum((product(weighted, spectra), contract(weighted, new_coeffs, 1, 1...  60.7 us
    psum x1, waiting for transfers between devices, local(): lax.psum((product(weighted, spectra), contract(weighted, new_coeffs, 1, 1...  28.7 us
    dot_general x6, matrix products, contract(): lax.dot_general(left, right, (((left_dim,), (right_dim,)), ((), ())), pre...  23.1 us
    dot_general x5, matrix products, product(): jnp.dot(left, right, precision=lax.Precision.HIGHEST, preferred_element_t...  17.9 us
    psum x1, waiting for transfers between devices, local(): numer_coeff, gram_all = lax.psum((local_numer, local_gram), 'chan')  16 us
    psum x1, blocking collectives, local(): numer_coeff, gram_all = lax.psum((local_numer, local_gram), 'chan')  9.69 us
    psum x1, blocking collectives, local(): lax.psum(contract(new_endmembers, new_endmembers, 1, 1), 'chan')  8.11 us
  transfers between devices with their start and end apart: 2, of which 2 were waited for; matrix products, arithmetic and copies ran while one was open for 1% of the time, Pallas kernels for 0%

commit v1 on v0

--- a/solution.py
+++ b/solution.py
@@ -43,7 +43,9 @@
     new_endmembers = endmembers * numer_end / (product(outer_gram, endmembers) + EPSILON)
     phase_means = phase_sums / (phase_counts + 1.0)[:, None]
     centroids = product(phase_means, new_endmembers)
-    gram_updated = lax.psum(contract(new_endmembers, new_endmembers, 1, 1), "chan")
+    gram_updated = jnp.sum(
+        lax.all_gather(contract(new_endmembers, new_endmembers, 1, 1), "chan"), axis=0
+    )
     offset = new_coeffs - contract(phase_means, onehot, 0, 0)
     distance = jnp.sum(offset * product(gram_updated, offset), axis=0) / channels_total
     return (new_coeffs, new_endmembers, centroids, distance)

time: 180 us -> 233 us (1.29)
  waiting for transfers between devices: 44.8 us -> 102 us
  blocking collectives: 78.5 us -> 74.7 us
    psum x1, waiting for transfers between devices: 28.7 us -> 85.8 us  [local(): lax.psum((product(weighted, spectra), contract(weighted, new_coeffs, 1, 1...]
    psum x1 -> x0, blocking collectives: 8.11 us -> none  [local(): lax.psum(contract(new_endmembers, new_endmembers, 1, 1), 'chan')]
    all_gather x0 -> x1, blocking collectives: none -> 4.39 us  [local(): lax.all_gather(contract(new_endmembers, new_endmembers, 1, 1), 'chan')]
  transfers between devices with their start and end apart: 2 -> 2, of which waited for: 2 -> 2; matrix products, arithmetic and copies ran while one was open for 1% -> 0% of each run, Pallas kernels for 0% -> 0%
where the time goes in v1:
time: 233 us
  waiting for transfers between devices  102 us (44%)
  blocking collectives  74.7 us (32%)
  matrix products  41 us (18%)
  between operations  14.2 us (6%)
    psum x1, waiting for transfers between devices, local(): lax.psum((product(weighted, spectra), contract(weighted, new_coeffs, 1, 1...  85.8 us
    psum x1, blocking collectives, local(): lax.psum((product(weighted, spectra), contract(weighted, new_coeffs, 1, 1...  60.7 us
    dot_general x6, matrix products, contract(): lax.dot_general(left, right, (((left_dim,), (right_dim,)), ((), ())), pre...  23.1 us
    dot_general x5, matrix products, product(): jnp.dot(left, right, precision=lax.Precision.HIGHEST, preferred_element_t...  17.9 us
    psum x1, waiting for transfers between devices, local(): numer_coeff, gram_all = lax.psum((local_numer, local_gram), 'chan')  16 us
    psum x1, blocking collectives, local(): numer_coeff, gram_all = lax.psum((local_numer, local_gram), 'chan')  9.69 us
  transfers between devices with their start and end apart: 2, of which 2 were waited for; matrix products, arithmetic and copies ran while one was open for 0% of the time, Pallas kernels for 0%

profile of v1, /device:TPU:0, one launch (start us, length us, event | category | flops | bytes accessed | tf_op | source)
XLA Modules:
  0.0 232.7 jit_solution(4842331529808148425)
XLA Ops:
  7.2 0.0 all-reduce.4.cloned.1.call-start
  7.3 21.4 %fusion.17 = f32[32,2048]{1,0:T(8,128)} fusion(f32[32,2048]{1,0:T(8,128)} %param.7, f32[2048,2048]{1,0:T(8,128)} %param.5), kind=kOutput, calls=%fused_computation.26 | convolution fusion | flops 1610612736 | bytes 17301504 | tf_op jit(solution)/shard_map/dot_general | solution.py:15
  28.6 0.0 all-reduce.4.cloned.1.call-update
  28.7 0.0 all-reduce.6.cloned.1.call-start
  28.7 0.4 fusion.18
  29.1 9.7 %psum.43 = f32[32,32]{1,0:T(8,128)S(1)} all-reduce(f32[32,32]{1,0:T(8,128)S(1)} %fusion.18), channel_id=1, replica_groups=mesh['pix'=16,'chan'=2] {'chan'}, use_global_device_ids=true, to_apply=%region_1.0 | all-reduce | flops 1024 | bytes 8192 | tf_op jit(solution)/shard_map/psum | solution.py:28
  38.8 0.1 select_reduce_fusion
  38.9 16.0 %all-reduce.4.cloned.1.call-done = f32[32,2048]{1,0:T(8,128)} async-done(((f32[32,2048]{1,0:T(8,128)}), f32[32,2048]{1,0:T(8,128)}) %all-reduce.4.cloned.1.call-update) | async-done | bytes 262160 | tf_op jit(solution)/shard_map/psum | solution.py:28
  54.9 1.3 fusion.1
  56.3 0.0 copy-start
  56.3 0.3 fusion.7
  56.6 0.4 fusion.3
  56.9 13.8 %fusion.5 = f32[32,2048]{1,0:T(8,128)} fusion(f32[2048,2048]{1,0:T(8,128)} %param.5, f32[32,2048]{1,0:T(8,128)S(1)} %fusion.1, f32[2048]{0:T(1024)S(1)} %convert_element_type.4), kind=kOutput, calls=%fused_computation.9 | convolution fusion | flops 1610678272 | bytes 17309696 | tf_op jit(solution)/shard_map/dot_general | solution.py:11
  70.8 60.7 %all-reduce = (f32[32,32]{1,0:T(8,128)S(1)}, f32[24,32]{1,0:T(8,128)S(1)}, f32[24]{0:T(128)S(1)}) all-reduce(f32[32,32]{1,0:T(8,128)S(1)} %fusion.3, f32[24,32]{1,0:T(8,128)S(1)} %fusion.7, f32[24]{0:T(128)S(1)} %select_reduce_fusion), channel_id=1, replica_groups=mesh['pix'=16,'chan'=2] {'pix'}, use_global_device_ids=true, to_apply=%region_3.0 | all-reduce | flops 1816 | bytes 14528 | tf_op jit(solution)/shard_map/psum | solution.py:34
  131.5 0.0 all-reduce.6.cloned.1.call-update
  131.5 0.4 convolution_subtract_fusion
  131.9 85.8 %all-reduce.6.cloned.1.call-done = f32[32,2048]{1,0:T(8,128)} async-done(((f32[32,2048]{1,0:T(8,128)}), f32[32,2048]{1,0:T(8,128)}) %all-reduce.6.cloned.1.call-update) | async-done | bytes 262160 | tf_op jit(solution)/shard_map/psum | solution.py:34
  217.7 1.3 fusion
  219.0 0.0 copy-start.2
  219.0 0.3 fusion.19
  219.4 1.1 fusion.15
  220.4 4.4 %all-gather = f32[64,32]{1,0:T(8,128)S(1)} all-gather(f32[32,32]{1,0:T(8,128)S(1)} %fusion.19), channel_id=2, replica_groups=mesh['pix'=16,'chan'=2] {'chan'}, dimensions={0}, use_global_device_ids=true | all-gather | bytes 12288 | tf_op jit(solution)/shard_map/all_gather | solution.py:47
  224.8 0.4 fusion.2
  225.2 0.6 broadcast_multiply_fusion
  (13 shorter events, 0.0 us)
Async XLA Ops:
  7.2 21.6 %copy-start.1 = (f32[32,2048]{1,0:T(8,128)S(1)}, f32[32,2048]{1,0:T(8,128)}, u32[]{:S(2)}) copy-start(f32[32,2048]{1,0:T(8,128)} %param.7) | copy-start | bytes 786436
  7.2 21.5 %copy-start.4 = (s32[2048]{0:T(1024)S(1)}, s32[2048]{0:T(1024)}, u32[]{:S(2)}) copy-start(s32[2048]{0:T(1024)} %param.8) | copy-start | bytes 24580
  7.2 31.6 %copy-start.3 = (s32[2048]{0:T(1024)S(1)}, s32[2048]{0:T(1024)}, u32[]{:S(2)}) copy-start(s32[2048]{0:T(1024)} %param.9) | copy-start | bytes 24580
  7.2 47.7 %copy-start.5 = (f32[32,2048]{1,0:T(8,128)S(1)}, f32[32,2048]{1,0:T(8,128)}, u32[]{:S(2)}) copy-start(f32[32,2048]{1,0:T(8,128)} %param.6) | copy-start | bytes 786436
  7.2 47.7 %all-reduce.4.cloned.1.call-start = ((), (), s32[]{:S(2)}) async-start(), calls=%async_computation | async-start | bytes 524288 | tf_op jit(solution)/shard_map/psum | solution.py:28
  28.7 189.0 %all-reduce.6.cloned.1.call-start = ((), (), s32[]{:S(2)}) async-start(), calls=%async_computation.1 | async-start | bytes 524288 | tf_op jit(solution)/shard_map/psum | solution.py:34
  56.3 169.6 %copy-start = (f32[32,2048]{1,0:T(8,128)}, f32[32,2048]{1,0:T(8,128)S(1)}, u32[]{:S(2)}) copy-start(f32[32,2048]{1,0:T(8,128)S(1)} %fusion.1) | copy-start | bytes 786436
  219.0 6.8 %copy-start.2 = (f32[32,2048]{1,0:T(8,128)}, f32[32,2048]{1,0:T(8,128)S(1)}, u32[]{:S(2)}) copy-start(f32[32,2048]{1,0:T(8,128)S(1)} %fusion) | copy-start | bytes 786436
Sparse Core Ops, SparseCore 0:
  28.8 26.0 all-reduce.3
  131.6 86.0 all-reduce.5
